TPU v7x, 32 devices: a whole 2x2x4 slice. The times are simulated.
32 devices in a mesh: row: 8 (over z, x), col: 4 (over y, core).
Axes of the slice: x: 2, y: 2, z: 4, core: 2. Of those that a mesh axis runs over, the one named last changes fastest.
Arguments:
- tokens: bfloat16 [4096, 768], P(('row', 'col')), may hold values from -6 to 6
- w_qkv: bfloat16 [768, 3, 768], P('row', None, 'col'), may hold values from -0.21875 to 0.21875
- w_out: bfloat16 [768, 768], P('col', 'row'), may hold values from -2.5 to 2.5
- w_gate_up: bfloat16 [768, 2, 3072], P('row', None, 'col'), may hold values from -0.21875 to 0.21875
- w_down: bfloat16 [3072, 768], P('col', 'row'), may hold values from -0.109375 to 0.109375
- gain1: float32 [768], replicated, may hold values from 0.1 to 1.9
- bias1: float32 [768], replicated, may hold values from -1.8 to 1.8
- gain2: float32 [768], replicated, may hold values from 0.1 to 1.9
- bias2: float32 [768], replicated, may hold values from -1.8 to 1.8
- cotangent: bfloat16 [4096, 768], P(('row', 'col')), may hold values from -6 to 6
- seq_lengths: int32 [3], replicated, may hold values from 512 to 2048, as said below
- packed_order: int32 [4096], replicated, may hold values from 0 to 4095, each once
Outputs:
- output: bfloat16 [4096, 768], P(('row', 'col'))
- grad_tokens: float32 [4096, 768], P(('row', 'col'))
- grad_w_qkv: float32 [768, 3, 768], P('row', None, 'col')
- grad_w_out: float32 [768, 768], P('col', 'row')
- grad_w_gate_up: float32 [768, 2, 3072], P('row', None, 'col')
- grad_w_down: float32 [3072, 768], P('col', 'row')
- grad_gain1: float32 [768], replicated
- grad_bias1: float32 [768], replicated
- grad_gain2: float32 [768], replicated
- grad_bias2: float32 [768], replicated
Inputs may be any that keep to these rules, and one draw needn't show every extreme that they name: `seq_lengths`: 3 lengths that sum to 4096; the longest is exactly 2048.
All inputs are finite; a program needn't handle non-finite values.
Results may differ from a plain program's by a relative error of at most 0.024.
Values may be sent and summed in bfloat16 or wider, within the bound.
No kernel may reach another device: no remote copies, remote signals or barrier semaphores. Data moves between devices by JAX's collectives and lax.ppermute only.
A program may use at most 512 MiB of HBM per device.

v0:
```python
import math
import jax
import jax.numpy as jnp
from jax import lax
from jax.sharding import PartitionSpec as P

HEAD = 64
ROPE_BASE = 1000.0
NORM_EPS = 1e-12
MASKED = -1e30


def token_layout(seq_lengths, packed_order):
    seq_ends = jnp.cumsum(seq_lengths)
    seq_starts = seq_ends - seq_lengths
    seq_id = jnp.sum((packed_order[:, None] >= seq_ends[None, :]).astype(jnp.int32), axis=1)
    member = seq_id[:, None] == jnp.arange(seq_lengths.shape[0], dtype=jnp.int32)[None, :]
    start_of = jnp.sum(jnp.where(member, seq_starts[None, :], 0), axis=1)
    return (seq_id, packed_order - start_of)


def rope_tables(positions, head):
    half = head // 2
    freqs = ROPE_BASE ** (-jnp.arange(half, dtype=jnp.float32) * 2.0 / head)
    angles = positions.astype(jnp.float32)[:, None] * freqs[None, :]
    return (jnp.cos(angles), jnp.sin(angles))


def rotate(field, cosine, sine):
    half = field.shape[-1] // 2
    first = field[..., :half]
    second = field[..., half:]
    cos_b = cosine[:, None, :]
    sin_b = sine[:, None, :]
    return jnp.concatenate(
        [first * cos_b - second * sin_b, second * cos_b + first * sin_b], axis=-1
    )


def rotate_back(field, cosine, sine):
    half = field.shape[-1] // 2
    first = field[..., :half]
    second = field[..., half:]
    cos_b = cosine[:, None, :]
    sin_b = sine[:, None, :]
    return jnp.concatenate(
        [first * cos_b + second * sin_b, second * cos_b - first * sin_b], axis=-1
    )


def norm_forward(values, gain, bias):
    centered = values - jnp.mean(values, axis=-1, keepdims=True)
    inverse = lax.rsqrt(jnp.mean(centered * centered, axis=-1, keepdims=True) + NORM_EPS)
    normed = centered * inverse
    return (normed * gain + bias, normed, inverse)


def norm_backward(grad_out, normed, inverse, gain):
    scaled = grad_out * gain
    grad_in = inverse * (
        scaled
        - jnp.mean(scaled, axis=-1, keepdims=True)
        - normed * jnp.mean(scaled * normed, axis=-1, keepdims=True)
    )
    return (grad_in, jnp.sum(grad_out * normed, axis=0), jnp.sum(grad_out, axis=0))


def gather_rows(rows):
    return lax.all_gather(rows, "col", axis=0, tiled=True)


def gather_grads(rows):
    return lax.all_gather(rows, "col", axis=0, tiled=True)


def column_sum(left, product):
    return lax.psum_scatter(
        product(left).astype(jnp.bfloat16), "col", scatter_dimension=0, tiled=True
    ).astype(jnp.float32)


def score_block(queries, seg_queries, key_rows, seg_keys, scale):
    count = key_rows.shape[0]
    heads = queries.shape[1]
    head = queries.shape[2]
    scores = (
        jnp.einsum(
            "qhd,khd->hqk",
            queries,
            key_rows.reshape(count, heads, head),
            preferred_element_type=jnp.float32,
        )
        * scale
    )
    same = seg_queries[:, None] == seg_keys[None, :]
    return (scores, same)


def probabilities(queries, seg_queries, log_total, key_rows, seg_keys, scale):
    scores, same = score_block(queries, seg_queries, key_rows, seg_keys, scale)
    return jnp.where(same[None], jnp.exp(scores - log_total[..., None]), 0.0)


def score_grads(probs, grad_heads, delta, value_rows):
    count = value_rows.shape[0]
    heads = grad_heads.shape[1]
    head = grad_heads.shape[2]
    grad_probs = jnp.einsum(
        "qhd,khd->hqk",
        grad_heads,
        value_rows.reshape(count, heads, head),
        preferred_element_type=jnp.float32,
    )
    return (probs * (grad_probs - delta[..., None])).astype(jnp.bfloat16)


def local(
    tokens,
    w_qkv,
    w_out,
    w_gate_up,
    w_down,
    gain1,
    bias1,
    gain2,
    bias2,
    cotangent,
    seq_lengths,
    packed_order,
):
    row_index = lax.axis_index("row")
    shards = lax.axis_size("row")
    full_qkv, full_out, full_gate_up, full_down = (
        lax.all_gather(w_qkv, "row", axis=0, tiled=True),
        lax.all_gather(w_out, "row", axis=1, tiled=True),
        lax.all_gather(w_gate_up, "row", axis=0, tiled=True),
        lax.all_gather(w_down, "row", axis=1, tiled=True),
    )
    seq_all, positions = token_layout(seq_lengths, packed_order)
    token_block = gather_rows(tokens)
    group = token_block.shape[0]
    first_slot = row_index * group
    seg_rows = lax.dynamic_slice_in_dim(seq_all, first_slot, group, 0)
    cosine, sine = rope_tables(lax.dynamic_slice_in_dim(positions, first_slot, group, 0), HEAD)
    width = full_qkv.shape[2]
    local_heads = width // HEAD
    scale = 1.0 / math.sqrt(HEAD)
    mixed = jnp.einsum("td,dce->tce", token_block, full_qkv, preferred_element_type=jnp.float32)
    query_bf = rotate(mixed[:, 0].reshape(group, local_heads, HEAD), cosine, sine).astype(
        jnp.bfloat16
    )
    key_bf = (
        rotate(mixed[:, 1].reshape(group, local_heads, HEAD), cosine, sine)
        .astype(jnp.bfloat16)
        .reshape(group, width)
    )
    value_bf = mixed[:, 2].astype(jnp.bfloat16)
    run_max = jnp.full((local_heads, group), MASKED, jnp.float32)
    key_piece = lax.all_gather(key_bf, "row", axis=0, tiled=True)
    value_piece = lax.all_gather(value_bf, "row", axis=0, tiled=True)
    count = key_piece.shape[0]
    seg_keys = seq_all
    scores, same = score_block(query_bf, seg_rows, key_piece, seg_keys, scale)
    new_max = jnp.maximum(run_max, jnp.max(jnp.where(same[None], scores, MASKED), axis=-1))
    weights_now = jnp.where(same[None], jnp.exp(scores - new_max[..., None]), 0.0)
    new_total = jnp.sum(weights_now, axis=-1)
    new_acc = jnp.einsum(
        "hqk,khd->hqd",
        weights_now.astype(jnp.bfloat16),
        value_piece.reshape(count, local_heads, HEAD),
        preferred_element_type=jnp.float32,
    )
    context = new_acc / new_total[..., None]
    log_total = new_max + jnp.log(new_total)
    context_bf = jnp.transpose(context, (1, 0, 2)).reshape(group, width).astype(jnp.bfloat16)

    def out_product(rows):
        return jnp.dot(rows, full_out, preferred_element_type=jnp.float32)

    attn_out = column_sum(context_bf, out_product)
    residual1 = tokens.astype(jnp.float32) + attn_out
    hidden1, normed1, inverse1 = norm_forward(residual1, gain1, bias1)
    hidden_block = gather_rows(hidden1.astype(jnp.bfloat16))
    gate_up = jnp.einsum(
        "td,dcf->tcf", hidden_block, full_gate_up, preferred_element_type=jnp.float32
    )
    up = gate_up[:, 0]
    gate = gate_up[:, 1]
    sigma = jax.nn.sigmoid(gate)
    inner = (gate * sigma * up).astype(jnp.bfloat16)

    def down_product(rows):
        return jnp.dot(rows, full_down, preferred_element_type=jnp.float32)

    ffn_out = column_sum(inner, down_product)
    residual2 = hidden1 + ffn_out
    result, normed2, inverse2 = norm_forward(residual2, gain2, bias2)
    grad_res2, grad_gain2, grad_bias2 = norm_backward(
        cotangent.astype(jnp.float32), normed2, inverse2, gain2
    )
    grad_ffn = gather_grads(grad_res2.astype(jnp.bfloat16))
    grad_inner = lax.dot_general(
        grad_ffn, full_down, (((1,), (1,)), ((), ())), preferred_element_type=jnp.float32
    )
    grad_down = lax.dot_general(
        inner, grad_ffn, (((0,), (0,)), ((), ())), preferred_element_type=jnp.float32
    )
    grad_up = grad_inner * gate * sigma
    grad_gate = grad_inner * up * sigma * (1.0 + gate * (1.0 - sigma))
    grad_gate_up = jnp.stack([grad_up, grad_gate], axis=1).astype(jnp.bfloat16)

    def gate_up_back(rows):
        return jnp.einsum("tcf,dcf->td", rows, full_gate_up, preferred_element_type=jnp.float32)

    grad_hidden1 = grad_res2 + column_sum(grad_gate_up, gate_up_back)
    grad_wgu = jnp.einsum(
        "td,tcf->dcf", hidden_block, grad_gate_up, preferred_element_type=jnp.float32
    )
    grad_res1, grad_gain1, grad_bias1 = norm_backward(grad_hidden1, normed1, inverse1, gain1)
    grad_attn = gather_grads(grad_res1.astype(jnp.bfloat16))
    grad_wo = lax.dot_general(
        context_bf, grad_attn, (((0,), (0,)), ((), ())), preferred_element_type=jnp.float32
    )
    grad_context_bf = lax.dot_general(
        grad_attn, full_out, (((1,), (1,)), ((), ())), preferred_element_type=jnp.float32
    ).astype(jnp.bfloat16)
    grad_heads = grad_context_bf.reshape(group, local_heads, HEAD)
    delta = jnp.sum(jnp.transpose(grad_heads, (1, 0, 2)).astype(jnp.float32) * context, axis=-1)
    key_all, value_all = (
        lax.all_gather(key_bf, "row", axis=0, tiled=True),
        lax.all_gather(value_bf, "row", axis=0, tiled=True),
    )
    tokens_total = key_all.shape[0]
    per_turn = group * math.gcd(shards, max(1, 2048 // group))
    turns = tokens_total // per_turn

    def turn_terms(turn):
        begin = turn * per_turn
        key_rows = lax.dynamic_slice_in_dim(key_all, begin, per_turn, 0)
        value_rows = lax.dynamic_slice_in_dim(value_all, begin, per_turn, 0)
        seg_keys = lax.dynamic_slice_in_dim(seq_all, begin, per_turn, 0)
        probs = probabilities(query_bf, seg_rows, log_total, key_rows, seg_keys, scale)
        grad_scores = score_grads(probs, grad_heads, delta, value_rows)
        return (begin, key_rows, probs, grad_scores)

    def query_term(grad_scores, key_rows):
        return jnp.einsum(
            "hqk,khd->qhd",
            grad_scores,
            key_rows.reshape(per_turn, local_heads, HEAD),
            preferred_element_type=jnp.float32,
        )

    empty_query = jnp.zeros((group, local_heads, HEAD), jnp.float32)

    def key_turn(turn, carry):
        grad_query, grad_keys, grad_values = carry
        begin, key_rows, probs, grad_scores = turn_terms(turn)
        grad_query = grad_query + query_term(grad_scores, key_rows)
        key_term = jnp.einsum(
            "hqk,qhd->khd", grad_scores, query_bf, preferred_element_type=jnp.float32
        ).reshape(per_turn, width)
        value_term = jnp.einsum(
            "hqk,qhd->khd",
            probs.astype(jnp.bfloat16),
            grad_heads,
            preferred_element_type=jnp.float32,
        ).reshape(per_turn, width)
        grad_keys = lax.dynamic_update_slice_in_dim(grad_keys, key_term, begin, 0)
        grad_values = lax.dynamic_update_slice_in_dim(grad_values, value_term, begin, 0)
        return (grad_query, grad_keys, grad_values)

    empty_keys = jnp.zeros((tokens_total, width), jnp.float32)
    grad_query, grad_keys_all, grad_values_all = lax.fori_loop(
        0, turns, key_turn, (empty_query, empty_keys, empty_keys)
    )
    grad_key_rows, grad_value_rows = (
        lax.psum_scatter(grad_keys_all, "row", scatter_dimension=0, tiled=True),
        lax.psum_scatter(grad_values_all, "row", scatter_dimension=0, tiled=True),
    )
    grad_query_raw = rotate_back(grad_query * scale, cosine, sine).reshape(group, width)
    grad_key_raw = rotate_back(
        grad_key_rows.reshape(group, local_heads, HEAD) * scale, cosine, sine
    ).reshape(group, width)
    grad_mixed = jnp.stack([grad_query_raw, grad_key_raw, grad_value_rows], axis=1).astype(
        jnp.bfloat16
    )

    def qkv_back(rows):
        return jnp.einsum("tce,dce->td", rows, full_qkv, preferred_element_type=jnp.float32)

    grad_tokens = grad_res1 + column_sum(grad_mixed, qkv_back)
    grad_wqkv = jnp.einsum(
        "td,tce->dce", token_block, grad_mixed, preferred_element_type=jnp.float32
    )
    grad_w_qkv, grad_w_out, grad_w_gate_up, grad_w_down = (
        lax.psum_scatter(grad_wqkv, "row", scatter_dimension=0, tiled=True),
        lax.psum_scatter(grad_wo, "row", scatter_dimension=1, tiled=True),
        lax.psum_scatter(grad_wgu, "row", scatter_dimension=0, tiled=True),
        lax.psum_scatter(grad_down, "row", scatter_dimension=1, tiled=True),
    )
    norm_gain1, norm_bias1, norm_gain2, norm_bias2 = lax.psum(
        (grad_gain1, grad_bias1, grad_gain2, grad_bias2), ("row", "col")
    )
    return (
        result.astype(jnp.bfloat16),
        grad_tokens,
        grad_w_qkv,
        grad_w_out,
        grad_w_gate_up,
        grad_w_down,
        norm_gain1,
        norm_bias1,
        norm_gain2,
        norm_bias2,
    )


def solution(mesh):
    placed = (
        P(("row", "col"), None),
        P("row", None, "col"),
        P("col", "row"),
        P("row", None, "col"),
        P("col", "row"),
        P(),
        P(),
        P(),
        P(),
        P(("row", "col"), None),
        P(),
        P(),
    )
    return jax.shard_map(
        local,
        mesh=mesh,
        in_specs=placed,
        out_specs=(
            P(("row", "col"), None),
            P(("row", "col"), None),
            P("row", None, "col"),
            P("col", "row"),
            P("row", None, "col"),
            P("col", "row"),
            P(),
            P(),
            P(),
            P(),
        ),
        check_vma=False,
    )
```

profile of v0, /device:TPU:0, one launch (start us, length us, event | category | flops | bytes accessed | tf_op | source)
XLA Modules:
  0.0 918.4 jit_solution(15256059629411682818)
XLA Ops:
  8.8 1.0 copy.45
  9.8 38.8 %all_gather.33 = bf16[768,3,192]{2,1,0:T(4,128)(2,1)S(1)} all-gather(bf16[96,3,192]{2,1,0:T(4,128)(2,1)S(1)} %copy.45), channel_id=1, replica_groups=mesh['row'=8,'col'=4] {'row'}, dimensions={0}, use_global_device_ids=true | all-gather | bytes 995328 | tf_op jit(solution)/shard_map/all_gather | solution.py:134
  49.5 8.8 all_gather.32
  62.9 1.3 broadcast_compare_fusion.1
  64.3 31.8 %all_gather.36 = bf16[192,768]{0,1:T(8,128)(2,1)S(1)} all-gather(bf16[192,96]{0,1:T(8,128)(2,1)S(1)} %copy.47), channel_id=1, replica_groups=mesh['row'=8,'col'=4] {'row'}, dimensions={1}, use_global_device_ids=true | all-gather | bytes 331776 | tf_op jit(solution)/shard_map/all_gather | solution.py:135
  96.1 11.8 %all-gather.6.cloned.1.call-done = bf16[4096,192]{0,1:T(8,128)(2,1)} async-done(((bf16[512,192]{0,1:T(8,128)(2,1)}), bf16[4096,192]{0,1:T(8,128)(2,1)}) %all-gather.6.cloned.1.call-update) | async-done | bytes 1572880 | tf_op jit(solution)/shard_map/all_gather | solution.py:159
  107.9 12.5 %select_reduce_fusion = (f32[3,512]{1,0:T(4,128)S(1)}, f32[3,512,4096]{2,1,0:T(8,128)}) fusion(pred[512,4096]{1,0:T(8,128)(4,1)S(1)} %broadcast_compare_fusion.1, bf16[4096,3,64]{0,2,1:T(8,128)(2,1)} %bitcast.162, bf16[512,3,32]{0,2,1:T(8,128)(2,1)S(1)} %get-tuple-element.336, bf16[512,3,32]{0,2,1:T(8,128)(2,1)S(1)} %get-tuple-element.335), kind=kOutput, calls=%fused_computation.16 | convolution fusion | flops 824572416 | bytes 29038592 | tf_op jit(solution)/shard_map/qhd,khd->hqk/dot_general | solution.py:87
  120.4 12.0 %fusion.8 = f32[3,512]{1,0:T(4,128)S(1)} fusion(f32[3,512,4096]{2,1,0:T(8,128)} %get-tuple-element.347, f32[3,512]{1,0:T(4,128)S(1)} %broadcast_maximum_fusion, pred[512,4096]{1,0:T(8,128)(4,1)S(1)} %broadcast_compare_fusion.1), kind=kLoop, calls=%fused_computation.17 | loop fusion | flops 25164288 | bytes 27275264 | tf_op jit(solution)/shard_map/reduce_sum | solution.py:166
  132.4 21.2 %all-gather.12.cloned.1.call-done = bf16[4096,1,192]{0,2,1:T(8,128)(2,1)} async-done(((bf16[512,1,192]{0,2,1:T(8,128)(2,1)}), bf16[4096,1,192]{0,2,1:T(8,128)(2,1)}) %all-gather.12.cloned.1.call-update) | async-done | bytes 1572880 | tf_op jit(solution)/shard_map/all_gather | solution.py:160
  153.6 12.0 %fusion.29 = (bf16[512,3,64]{0,2,1:T(8,128)(2,1)S(1)}, f32[3,512,64]{1,2,0:T(8,128)}) fusion(f32[512,3]{0,1:T(4,128)S(1)} %bitcast.183, bf16[4096,3,64]{0,2,1:T(8,128)(2,1)} %bitcast.163, f32[3,512,4096]{2,1,0:T(8,128)} %get-tuple-element.347, f32[3,512]{1,0:T(4,128)S(1)} %broadcast_maximum_fusion, pred[512,4096]{1,0:T(8,128)(4,1)S(1)} %broadcast_compare_fusion.1), kind=kOutput, calls=%fused_computation.58 | convolution fusion | flops 830668800 | bytes 29437952 | tf_op jit(solution)/shard_map/hqk,khd->hqd/dot_general | solution.py:167
  165.6 1.3 convolution_convert_fusion.1
  167.0 1.7 copy.48
  169.4 19.2 %reduce-scatter.15.cloned.1.call-done = bf16[128,768]{1,0:T(8,128)(2,1)} async-done(((bf16[512,768]{1,0:T(8,128)(2,1)}), bf16[128,768]{1,0:T(8,128)(2,1)}) %reduce-scatter.15.cloned.1.call-update) | async-done | bytes 196624 | tf_op jit(solution)/shard_map/reduce_scatter | solution.py:77
  188.6 1.1 fusion.31
  189.6 1.1 multiply_reduce_fusion.3
  190.8 1.1 fusion.33
  191.8 8.4 all_gather.37
  200.2 43.2 %all-gather.8.cloned.1.call-done = bf16[768,2,768]{2,0,1:T(8,128)(2,1)} async-done(((bf16[96,2,768]{2,0,1:T(8,128)(2,1)}), bf16[768,2,768]{2,0,1:T(8,128)(2,1)}) %all-gather.8.cloned.1.call-update) | async-done | bytes 2359312 | tf_op jit(solution)/shard_map/all_gather | solution.py:136
  243.4 3.0 fusion.17
  246.5 1.6 copy-done.11
  248.6 36.7 %all-gather.10.cloned.1.call-done = bf16[768,768]{0,1:T(8,128)(2,1)} async-done(((bf16[768,96]{0,1:T(8,128)(2,1)}), bf16[768,768]{0,1:T(8,128)(2,1)}) %all-gather.10.cloned.1.call-update) | async-done | bytes 1179664 | tf_op jit(solution)/shard_map/all_gather | solution.py:137
  285.3 3.0 convolution_convert_fusion
  288.3 22.1 %reduce-scatter.17.cloned.1.call-done = bf16[128,768]{1,0:T(8,128)(2,1)} async-done(((bf16[512,768]{1,0:T(8,128)(2,1)}), bf16[128,768]{1,0:T(8,128)(2,1)}) %reduce-scatter.17.cloned.1.call-update) | async-done | bytes 196624 | tf_op jit(solution)/shard_map/reduce_scatter | solution.py:77
  310.5 1.3 fusion.46
  313.7 8.2 all_gather.40
  321.9 2.7 fusion.19
  325.8 2.3 bitcast_convert_fusion.1
  328.2 23.7 %reduce-scatter.19.cloned.1.call-done = bf16[128,768]{1,0:T(8,128)(2,1)} async-done(((bf16[512,768]{1,0:T(8,128)(2,1)}), bf16[128,768]{1,0:T(8,128)(2,1)}) %reduce-scatter.19.cloned.1.call-update) | async-done | bytes 196624 | tf_op jit(solution)/shard_map/reduce_scatter | solution.py:77
  352.0 1.2 multiply_reduce_fusion
  353.2 1.9 fusion.43
  355.1 8.2 all_gather.41
  364.2 2.0 broadcast_in_dim.122
  366.2 2.0 broadcast_in_dim.122.clone
  368.2 58.9 %while.18 = (s32[]{:T(128)}, f32[512,3,64]{0,2,1:T(8,128)S(1)}, f32[4096,192]{0,1:T(8,128)}, f32[4096,192]{0,1:T(8,128)}, bf16[4096,192]{0,1:T(8,128)(2,1)S(1)},...) while((s32[]{:T(128)}, f32[512,3,64]{0,2,1:T(8,128)S(1)}, ...), condition=%wide.region_18.19_spmd.clone, body=%wide.region_17.18_spmd.clone.sunk | while | flops 2045968384 | bytes 107786520 | solution.py:274
  368.3 6.4 fusion.105
  375.5 7.4 fusion.106
  382.9 2.0 fusion.109
  385.5 6.1 fusion.108
  391.6 2.1 constant_dynamic-update-slice_fusion.3
  393.6 4.0 fusion.107
  397.8 6.4 fusion.105
  404.9 7.4 fusion.106
  412.3 2.0 fusion.109
  414.9 6.1 fusion.108
  421.0 2.1 constant_dynamic-update-slice_fusion.3
  423.1 4.0 fusion.107
  428.3 1.4 convolution_bitcast_fusion.1
  429.8 4.7 fusion.13
  434.6 68.0 %reduce-scatter.21.cloned.1.call-done = f32[512,192]{0,1:T(8,128)} async-done(((f32[4096,192]{0,1:T(8,128)}), f32[512,192]{0,1:T(8,128)}) %reduce-scatter.21.cloned.1.call-update) | async-done | bytes 393232 | tf_op jit(solution)/shard_map/reduce_scatter | solution.py:278
  503.8 76.9 %reduce-scatter.23.cloned.1.call-done = f32[512,192]{0,1:T(8,128)} async-done(((f32[4096,192]{0,1:T(8,128)}), f32[512,192]{0,1:T(8,128)}) %reduce-scatter.23.cloned.1.call-update) | async-done | bytes 393232 | tf_op jit(solution)/shard_map/reduce_scatter | solution.py:279
  582.4 1.7 bitcast_convert_fusion
  584.5 1.7 fusion.14
  586.2 1.8 copy.62
  588.2 2.3 fusion.51
  590.5 40.1 %all-reduce = (f32[768]{0:T(1024)}, f32[768]{0:T(1024)}, f32[768]{0:T(1024)}, f32[768]{0:T(1024)}) all-reduce(f32[768]{0:T(1024)S(1)} %get-tuple-element.283, f32[768]{0:T(1024)S(1)} %get-tuple-element.288, f32[768]{0:T(1024)S(1)} %copy-done.34, f32[768]{0:T(1024)S(1)} %copy-done.35), channel_id=1, replica_groups=mesh['row'=8,'col'=4] {'row','col'}, use_global_device_ids=true, to_apply=%region_27.28 | all-reduce | flops 3072 | bytes 24576 | tf_op jit(solution)/shard_map/psum | solution.py:302
  630.6 15.3 %reduce-scatter.33.cloned.1.call-done = f32[96,192]{1,0:T(8,128)} async-done(((f32[768,192]{1,0:T(8,128)}), f32[96,192]{1,0:T(8,128)}) %reduce-scatter.33.cloned.1.call-update) | async-done | bytes 73744
  645.9 1.6 copy.61
  647.6 96.2 %reduce-scatter.27.cloned.1.call-done = f32[96,2,768]{2,0,1:T(8,128)} async-done(((f32[768,2,768]{2,0,1:T(8,128)}), f32[96,2,768]{2,0,1:T(8,128)}) %reduce-scatter.27.cloned.1.call-update) | async-done | bytes 589840 | tf_op jit(solution)/shard_map/reduce_scatter | solution.py:299
  743.8 2.3 copy.52
  746.1 23.1 %reduce-scatter.25.cloned.1.call-done = bf16[128,768]{1,0:T(8,128)(2,1)} async-done(((bf16[512,768]{1,0:T(8,128)(2,1)}), bf16[128,768]{1,0:T(8,128)(2,1)}) %reduce-scatter.25.cloned.1.call-update) | async-done | bytes 196624 | tf_op jit(solution)/shard_map/reduce_scatter | solution.py:77
  769.3 1.7 convert_add_fusion
  771.0 69.1 %reduce-scatter.31.cloned.1.call-done = f32[96,576]{1,0:T(8,128)} async-done(((f32[768,576]{1,0:T(8,128)}), f32[96,576]{1,0:T(8,128)}) %reduce-scatter.31.cloned.1.call-update) | async-done | bytes 221200
  840.0 1.1 copy.63
  842.0 69.8 %reduce-scatter.29.cloned.1.call-done = f32[768,96]{0,1:T(8,128)} async-done(((f32[768,768]{0,1:T(8,128)}), f32[768,96]{0,1:T(8,128)}) %reduce-scatter.29.cloned.1.call-update) | async-done | bytes 294928 | tf_op jit(solution)/shard_map/reduce_scatter | solution.py:300
  (160 shorter events, 20.6 us)
Async XLA Ops:
  7.2 42.3 %copy-start.3 = (bf16[128,768]{1,0:T(8,128)(2,1)S(1)}, bf16[128,768]{1,0:T(8,128)(2,1)}, u32[]{:S(2)}) copy-start(bf16[128,768]{1,0:T(8,128)(2,1)} %param.14) | copy-start | bytes 589828
  7.2 100.7 %all-gather.6.cloned.1.call-start = ((), (), s32[]{:S(2)}) async-start(), calls=%async_computation.10 | async-start | bytes 1769472 | tf_op jit(solution)/shard_map/all_gather | solution.py:159
  49.5 11.2 %copy-start.9 = (bf16[768,3,192]{0,2,1:T(8,128)(2,1)}, bf16[768,3,192]{0,2,1:T(8,128)(2,1)S(1)}, u32[]{:S(2)}) copy-start(bf16[768,3,192]{0,2,1:T(8,128)(2,1)S(1)} %copy.46) | copy-start | bytes 2654212
  49.5 10.4 %copy-start.31 = (s32[4096]{0:T(1024)S(1)}, s32[4096]{0:T(1024)}, u32[]{:S(2)}) copy-start(s32[4096]{0:T(1024)} %param.25) | copy-start | bytes 49156
  58.3 0.9 copy-start.13
  59.9 4.3 copy-start.30
  60.6 0.6 copy-start.21
  60.6 0.6 copy-start.23
  62.0 91.6 %all-gather.12.cloned.1.call-start = ((), (), s32[]{:S(2)}) async-start(), calls=%async_computation.21 | async-start | bytes 1769472 | tf_op jit(solution)/shard_map/all_gather | solution.py:160
  62.7 125.8 %reduce-scatter.15.cloned.1.call-start = ((), (), s32[]{:S(2)}) async-start(), calls=%async_computation.11 | async-start | bytes 983040 | tf_op jit(solution)/shard_map/reduce_scatter | solution.py:77
  165.6 25.1 %copy-start.29 = (f32[768]{0:T(1024)S(1)}, f32[768]{0:T(1024)}, u32[]{:S(2)}) copy-start(f32[768]{0:T(1024)} %param.19) | copy-start | bytes 9220
  165.6 25.1 %copy-start.32 = (f32[768]{0:T(1024)S(1)}, f32[768]{0:T(1024)}, u32[]{:S(2)}) copy-start(f32[768]{0:T(1024)} %param.20) | copy-start | bytes 9220
  167.0 76.4 %all-gather.8.cloned.1.call-start = ((), (), s32[]{:S(2)}) async-start(), calls=%async_computation.12 | async-start | bytes 2654208 | tf_op jit(solution)/shard_map/all_gather | solution.py:136
  168.8 116.5 %all-gather.10.cloned.1.call-start = ((), (), s32[]{:S(2)}) async-start(), calls=%async_computation.13 | async-start | bytes 1327104 | tf_op jit(solution)/shard_map/all_gather | solution.py:137
  169.3 141.1 %reduce-scatter.17.cloned.1.call-start = ((), (), s32[]{:S(2)}) async-start(), calls=%async_computation.14 | async-start | bytes 983040 | tf_op jit(solution)/shard_map/reduce_scatter | solution.py:77
  200.2 43.2 %copy-start.18 = (bf16[512,768]{1,0:T(8,128)(2,1)}, bf16[512,768]{1,0:T(8,128)(2,1)S(1)}, u32[]{:S(2)}) copy-start(bf16[512,768]{1,0:T(8,128)(2,1)S(1)} %all_gather.37) | copy-start | bytes 2359300
  246.5 1.6 copy-start.11
  248.6 64.2 %copy-start.7 = (bf16[512,768]{1,0:T(8,128)(2,1)}, bf16[512,768]{1,0:T(8,128)(2,1)S(1)}, u32[]{:S(2)}) copy-start(bf16[512,768]{1,0:T(8,128)(2,1)S(1)} %multiply_convert_fusion.2) | copy-start | bytes 2359300
  248.6 61.9 %copy-start.6 = (bf16[128,768]{1,0:T(8,128)(2,1)S(1)}, bf16[128,768]{1,0:T(8,128)(2,1)}, u32[]{:S(2)}) copy-start(bf16[128,768]{1,0:T(8,128)(2,1)} %reduce-scatter.15.cloned.1.call-done) | copy-start | bytes 589828
  248.6 63.4 %copy-start.20 = (bf16[128,768]{1,0:T(8,128)(2,1)S(1)}, bf16[128,768]{1,0:T(8,128)(2,1)}, u32[]{:S(2)}) copy-start(bf16[128,768]{1,0:T(8,128)(2,1)} %param.23) | copy-start | bytes 589828
  248.6 63.4 %copy-start.33 = (f32[768]{0:T(1024)S(1)}, f32[768]{0:T(1024)}, u32[]{:S(2)}) copy-start(f32[768]{0:T(1024)} %param.21) | copy-start | bytes 9220
  248.6 64.2 %copy-start.36 = (f32[768]{0:T(1024)S(1)}, f32[768]{0:T(1024)}, u32[]{:S(2)}) copy-start(f32[768]{0:T(1024)} %param.22) | copy-start | bytes 9220
  288.3 63.7 %reduce-scatter.19.cloned.1.call-start = ((), (), s32[]{:S(2)}) async-start(), calls=%async_computation.15 | async-start | bytes 983040 | tf_op jit(solution)/shard_map/reduce_scatter | solution.py:77
  310.5 11.4 %copy-start.12 = (f32[512,2,768]{2,0,1:T(8,128)S(1)}, f32[512,2,768]{2,0,1:T(8,128)}, u32[]{:S(2)}) copy-start(f32[512,2,768]{2,0,1:T(8,128)} %copy-done.11) | copy-start | bytes 9437188
  321.9 2.7 copy-start.15
  321.9 3.9 copy-start.37
  324.6 0.9 copy-start.38
  324.7 1.1 copy-start.40
  328.1 35.6 %copy-start.25 = (f32[3,512,64]{1,2,0:T(8,128)S(1)}, f32[3,512,64]{1,2,0:T(8,128)}, u32[]{:S(2)}) copy-start(f32[3,512,64]{1,2,0:T(8,128)} %get-tuple-element.349) | copy-start | bytes 1179652
  328.1 174.4 %reduce-scatter.21.cloned.1.call-start = ((), (), s32[]{:S(2)}) async-start(), calls=%async_computation.16 | async-start | bytes 3538944 | tf_op jit(solution)/shard_map/reduce_scatter | solution.py:278
  363.3 0.9 copy-start.4
  364.2 4.0 copy-start.1
  368.3 7.1 copy-start.2
  382.9 2.6 copy-start
  397.7 7.1 copy-start.2
  412.3 2.6 copy-start
  427.1 1.1 copy-start.5
  427.2 2.6 copy-start.19
  427.2 2.6 copy-start.39
  427.2 153.5 %reduce-scatter.23.cloned.1.call-start = ((), (), s32[]{:S(2)}) async-start(), calls=%async_computation.17 | async-start | bytes 3538944 | tf_op jit(solution)/shard_map/reduce_scatter | solution.py:279
  427.9 218.0 %reduce-scatter.33.cloned.1.call-start = ((), (), s32[]{:S(2)}) async-start(), calls=%async_computation.23 | async-start | bytes 884736
  429.7 314.1 %reduce-scatter.27.cloned.1.call-start = ((), (), s32[]{:S(2)}) async-start(), calls=%async_computation.19 | async-start | bytes 5308416 | tf_op jit(solution)/shard_map/reduce_scatter | solution.py:299
  434.5 69.1 %copy-start.22 = (f32[512,32]{0,1:T(8,128)S(1)}, f32[512,32]{0,1:T(8,128)}, u32[]{:S(2)}) copy-start(f32[512,32]{0,1:T(8,128)} %copy-done.21) | copy-start | bytes 196612
  434.5 69.1 %copy-start.24 = (f32[512,32]{0,1:T(8,128)S(1)}, f32[512,32]{0,1:T(8,128)}, u32[]{:S(2)}) copy-start(f32[512,32]{0,1:T(8,128)} %copy-done.23) | copy-start | bytes 196612
  434.5 147.9 %copy-start.10 = (bf16[768,3,192]{0,2,1:T(8,128)(2,1)S(1)}, bf16[768,3,192]{0,2,1:T(8,128)(2,1)}, u32[]{:S(2)}) copy-start(bf16[768,3,192]{0,2,1:T(8,128)(2,1)} %copy-done.9) | copy-start | bytes 2654212
  434.5 334.8 %reduce-scatter.25.cloned.1.call-start = ((), (), s32[]{:S(2)}) async-start(), calls=%async_computation.18 | async-start | bytes 983040 | tf_op jit(solution)/shard_map/reduce_scatter | solution.py:77
  503.7 80.4 %copy-start.26 = (bf16[512,3,64]{0,2,1:T(8,128)(2,1)}, bf16[512,3,64]{0,2,1:T(8,128)(2,1)S(1)}, u32[]{:S(2)}) copy-start(bf16[512,3,64]{0,2,1:T(8,128)(2,1)S(1)} %pad_maximum_fusion.8) | copy-start | bytes 589828
  503.8 80.7 %copy-start.14 = (bf16[512,768]{1,0:T(8,128)(2,1)S(1)}, bf16[512,768]{1,0:T(8,128)(2,1)}, u32[]{:S(2)}) copy-start(bf16[512,768]{1,0:T(8,128)(2,1)} %copy-done.13) | copy-start | bytes 2359300
  503.8 80.4 %copy-start.27 = (bf16[512,3,64]{0,2,1:T(8,128)(2,1)}, bf16[512,3,64]{0,2,1:T(8,128)(2,1)S(1)}, u32[]{:S(2)}) copy-start(bf16[512,3,64]{0,2,1:T(8,128)(2,1)S(1)} %pad_maximum_fusion.9) | copy-start | bytes 589828
  581.7 0.7 copy-start.28
  584.2 255.8 %reduce-scatter.31.cloned.1.call-start = ((), (), s32[]{:S(2)}) async-start(), calls=%async_computation.22 | async-start | bytes 2211840
  586.2 2.0 copy-start.8
  586.2 2.0 copy-start.16
  588.1 2.4 copy-start.34
  588.1 2.4 copy-start.35
  588.1 323.7 %reduce-scatter.29.cloned.1.call-start = ((), (), s32[]{:S(2)}) async-start(), calls=%async_computation.20 | async-start | bytes 2654208 | tf_op jit(solution)/shard_map/reduce_scatter | solution.py:300
  590.5 178.8 %copy-start.17 = (f32[128,768]{1,0:T(8,128)S(1)}, f32[128,768]{1,0:T(8,128)}, u32[]{:S(2)}) copy-start(f32[128,768]{1,0:T(8,128)} %get-tuple-element.320) | copy-start | bytes 1179652
Sparse Core Ops, SparseCore 0:
  62.1 45.7 all-gather.5
  110.5 43.0 all-gather.11
  167.1 21.4 reduce-scatter.14
  191.4 51.9 all-gather.7
  245.7 39.5 all-gather.9
  288.4 22.0 reduce-scatter.16
  328.3 23.6 reduce-scatter.18
  427.3 75.2 reduce-scatter.20
  506.6 74.0 reduce-scatter.22
  584.2 61.6 reduce-scatter.32
  649.6 94.1 reduce-scatter.26
  746.2 23.0 reduce-scatter.24
  773.1 66.8 reduce-scatter.30
  843.9 67.8 reduce-scatter.28
where the time goes:
time: 919 us; the launch traced here: 918 us
  waiting for transfers between devices  598 us (65%)
  blocking collectives  144 us (16%)
  matrix products  101 us (11%)
  other arithmetic  31.8 us (3%)
  local copies, waits for them, and re-layouts  27.6 us (3%)
  between operations  14.5 us (2%)
    reduce_scatter x1, waiting for transfers between devices, local(): lax.psum_scatter(grad_wgu, 'row', scatter_dimension=0, tiled=True)  96.2 us
    reduce_scatter x4, waiting for transfers between devices, column_sum(): lax.psum_scatter(product(left).astype(jnp.bfloat16), 'col', scatter_dimen...  88.2 us
    unnamed x16, waiting for transfers between devices  85.8 us
    reduce_scatter x1, waiting for transfers between devices, local(): lax.psum_scatter(grad_values_all, 'row', scatter_dimension=0, tiled=True)  76.9 us
    reduce_scatter x1, waiting for transfers between devices, local(): lax.psum_scatter(grad_down, 'row', scatter_dimension=1, tiled=True)  69.8 us
    reduce_scatter x1, waiting for transfers between devices, local(): lax.psum_scatter(grad_keys_all, 'row', scatter_dimension=0, tiled=True)  68 us
    all_gather x1, waiting for transfers between devices, local(): lax.all_gather(w_gate_up, 'row', axis=0, tiled=True)  43.2 us
    psum x1, blocking collectives, local(): lax.psum((grad_gain1, grad_bias1, grad_gain2, grad_bias2), ('row', 'col'))  40.1 us
  transfers between devices with their start and end apart: 14, of which 14 were waited for; matrix products, arithmetic and copies ran while one was open for 6% of the time, Pallas kernels for 0%

commit v1 on v0

--- a/solution.py
+++ b/solution.py
@@ -8,6 +8,14 @@
 ROPE_BASE = 1000.0
 NORM_EPS = 1e-12
 MASKED = -1e30
+
+
+def test_digits(row_data, dev_axis):
+    in_order = []
+    for _ in range(lax.psum(1, dev_axis)):
+        in_order.append(row_data)
+    vec_out = jnp.concatenate(lax.all_to_all(jnp.stack(in_order), dev_axis, 0, 0), axis=1)
+    return vec_out
 
 
 def token_layout(seq_lengths, packed_order):
@@ -132,7 +140,7 @@
     shards = lax.axis_size("row")
     full_qkv, full_out, full_gate_up, full_down = (
         lax.all_gather(w_qkv, "row", axis=0, tiled=True),
-        lax.all_gather(w_out, "row", axis=1, tiled=True),
+        test_digits(w_out, "row"),
         lax.all_gather(w_gate_up, "row", axis=0, tiled=True),
         lax.all_gather(w_down, "row", axis=1, tiled=True),
     )

time: 919 us -> 922 us (level)
  blocking collectives: 144 us -> 112 us
  waiting for transfers between devices: 598 us -> 628 us
    all_gather x1 -> x0, blocking collectives: 31.8 us -> none  [local(): lax.all_gather(w_out, 'row', axis=1, tiled=True)]
    all_to_all x0 -> x1, waiting for transfers between devices: none -> 15.9 us  [test_digits(): lax.all_to_all(jnp.stack(in_order), dev_axis, 0, 0)]
    all_gather x1, waiting for transfers between devices: 11.8 us -> 24 us  [local(): key_piece = lax.all_gather(key_bf, 'row', axis=0, tiled=True)]
  transfers between devices with their start and end apart: 14 -> 15, of which waited for: 14 -> 15; matrix products, arithmetic and copies ran while one was open for 6% -> 6% of each run, Pallas kernels for 0% -> 0%
where the time goes in v1:
time: 922 us; the launch traced here: 920 us
  waiting for transfers between devices  628 us (68%)
  blocking collectives  112 us (12%)
  matrix products  102 us (11%)
  other arithmetic  31.8 us (3%)
  local copies, waits for them, and re-layouts  27.9 us (3%)
  between operations  14.6 us (2%)
    reduce_scatter x1, waiting for transfers between devices, local(): lax.psum_scatter(grad_wgu, 'row', scatter_dimension=0, tiled=True)  96.5 us
    reduce_scatter x4, waiting for transfers between devices, column_sum(): lax.psum_scatter(product(left).astype(jnp.bfloat16), 'col', scatter_dimen...  89.1 us
    unnamed x16, waiting for transfers between devices  85.8 us
    reduce_scatter x1, waiting for transfers between devices, local(): lax.psum_scatter(grad_values_all, 'row', scatter_dimension=0, tiled=True)  77 us
    reduce_scatter x1, waiting for transfers between devices, local(): lax.psum_scatter(grad_down, 'row', scatter_dimension=1, tiled=True)  69.8 us
    reduce_scatter x1, waiting for transfers between devices, local(): lax.psum_scatter(grad_keys_all, 'row', scatter_dimension=0, tiled=True)  68.1 us
    all_gather x1, waiting for transfers between devices, local(): lax.all_gather(w_gate_up, 'row', axis=0, tiled=True)  43.2 us
    psum x1, blocking collectives, local(): lax.psum((grad_gain1, grad_bias1, grad_gain2, grad_bias2), ('row', 'col'))  40 us
  transfers between devices with their start and end apart: 15, of which 15 were waited for; matrix products, arithmetic and copies ran while one was open for 6% of the time, Pallas kernels for 0%

profile of v1, /device:TPU:0, one launch (start us, length us, event | category | flops | bytes accessed | tf_op | source)
XLA Modules:
  0.0 920.5 jit_solution(11304103595296093286)
XLA Ops:
  8.8 1.0 copy.54
  9.8 38.8 %all_gather.30 = bf16[768,3,192]{2,1,0:T(4,128)(2,1)S(1)} all-gather(bf16[96,3,192]{2,1,0:T(4,128)(2,1)S(1)} %copy.54), channel_id=1, replica_groups=mesh['row'=8,'col'=4] {'row'}, dimensions={0}, use_global_device_ids=true | all-gather | bytes 995328 | tf_op jit(solution)/shard_map/all_gather | solution.py:142
  49.5 8.8 all_gather.29
  62.8 3.7 all-to-all-start
  67.4 1.3 broadcast_compare_fusion.1
  68.7 15.9 %all-to-all-done = bf16[8,192,96]{2,1,0:T(8,128)(2,1)S(1)} async-done(((bf16[8,192,96]{2,1,0:T(8,128)(2,1)}), bf16[8,192,96]{2,1,0:T(8,128)(2,1)S(1)}, u32[]{:S(2)}, u32[]{:S(2)}) %all-to-all-start) | async-done | bytes 294944 | tf_op jit(solution)/shard_map/all_to_all | solution.py:17
  85.2 24.0 %all-gather.6.cloned.1.call-done = bf16[4096,192]{0,1:T(8,128)(2,1)} async-done(((bf16[512,192]{0,1:T(8,128)(2,1)}), bf16[4096,192]{0,1:T(8,128)(2,1)}) %all-gather.6.cloned.1.call-update) | async-done | bytes 1572880 | tf_op jit(solution)/shard_map/all_gather | solution.py:167
  109.3 12.6 %select_reduce_fusion = (f32[3,512]{1,0:T(4,128)S(1)}, f32[3,512,4096]{2,1,0:T(8,128)}) fusion(pred[512,4096]{1,0:T(8,128)(4,1)S(1)} %broadcast_compare_fusion.1, bf16[4096,3,64]{0,2,1:T(8,128)(2,1)} %bitcast.163, bf16[512,3,32]{0,2,1:T(8,128)(2,1)S(1)} %get-tuple-element.346, bf16[512,3,32]{0,2,1:T(8,128)(2,1)S(1)} %get-tuple-element.345), kind=kOutput, calls=%fused_computation.16 | convolution fusion | flops 824572416 | bytes 29038592 | tf_op jit(solution)/shard_map/qhd,khd->hqk/dot_general | solution.py:95
  121.9 12.0 %fusion.8 = f32[3,512]{1,0:T(4,128)S(1)} fusion(f32[3,512,4096]{2,1,0:T(8,128)} %get-tuple-element.357, f32[3,512]{1,0:T(4,128)S(1)} %broadcast_maximum_fusion, pred[512,4096]{1,0:T(8,128)(4,1)S(1)} %broadcast_compare_fusion.1), kind=kLoop, calls=%fused_computation.17 | loop fusion | flops 25164288 | bytes 27275264 | tf_op jit(solution)/shard_map/reduce_sum | solution.py:174
  133.8 21.6 %all-gather.12.cloned.1.call-done = bf16[4096,1,192]{0,2,1:T(8,128)(2,1)} async-done(((bf16[512,1,192]{0,2,1:T(8,128)(2,1)}), bf16[4096,1,192]{0,2,1:T(8,128)(2,1)}) %all-gather.12.cloned.1.call-update) | async-done | bytes 1572880 | tf_op jit(solution)/shard_map/all_gather | solution.py:168
  155.4 12.1 %fusion.29 = (bf16[512,3,64]{0,2,1:T(8,128)(2,1)S(1)}, f32[3,512,64]{1,2,0:T(8,128)}) fusion(f32[512,3]{0,1:T(4,128)S(1)} %bitcast.185, bf16[4096,3,64]{0,2,1:T(8,128)(2,1)} %bitcast.164, f32[3,512,4096]{2,1,0:T(8,128)} %get-tuple-element.357, f32[3,512]{1,0:T(4,128)S(1)} %broadcast_maximum_fusion, pred[512,4096]{1,0:T(8,128)(4,1)S(1)} %broadcast_compare_fusion.1), kind=kOutput, calls=%fused_computation.58 | convolution fusion | flops 830668800 | bytes 29437952 | tf_op jit(solution)/shard_map/hqk,khd->hqd/dot_general | solution.py:175
  167.5 1.3 convolution_convert_fusion.1
  170.3 20.1 %reduce-scatter.15.cloned.1.call-done = bf16[128,768]{1,0:T(8,128)(2,1)} async-done(((bf16[512,768]{1,0:T(8,128)(2,1)}), bf16[128,768]{1,0:T(8,128)(2,1)}) %reduce-scatter.15.cloned.1.call-update) | async-done | bytes 196624 | tf_op jit(solution)/shard_map/reduce_scatter | solution.py:85
  190.5 1.1 fusion.31
  191.5 1.1 multiply_reduce_fusion.3
  192.7 1.1 fusion.33
  193.7 8.4 all_gather.33
  202.1 43.2 %all-gather.8.cloned.1.call-done = bf16[768,2,768]{2,0,1:T(8,128)(2,1)} async-done(((bf16[96,2,768]{2,0,1:T(8,128)(2,1)}), bf16[768,2,768]{2,0,1:T(8,128)(2,1)}) %all-gather.8.cloned.1.call-update) | async-done | bytes 2359312 | tf_op jit(solution)/shard_map/all_gather | solution.py:144
  245.3 3.0 fusion.17
  248.4 1.6 copy-done.11
  250.5 36.7 %all-gather.10.cloned.1.call-done = bf16[768,768]{0,1:T(8,128)(2,1)} async-done(((bf16[768,96]{0,1:T(8,128)(2,1)}), bf16[768,768]{0,1:T(8,128)(2,1)}) %all-gather.10.cloned.1.call-update) | async-done | bytes 1179664 | tf_op jit(solution)/shard_map/all_gather | solution.py:145
  287.2 3.0 convolution_convert_fusion
  290.2 22.1 %reduce-scatter.17.cloned.1.call-done = bf16[128,768]{1,0:T(8,128)(2,1)} async-done(((bf16[512,768]{1,0:T(8,128)(2,1)}), bf16[128,768]{1,0:T(8,128)(2,1)}) %reduce-scatter.17.cloned.1.call-update) | async-done | bytes 196624 | tf_op jit(solution)/shard_map/reduce_scatter | solution.py:85
  312.4 1.3 fusion.46
  315.6 8.2 all_gather.36
  323.8 2.7 fusion.19
  327.7 2.3 bitcast_convert_fusion.1
  330.2 23.7 %reduce-scatter.19.cloned.1.call-done = bf16[128,768]{1,0:T(8,128)(2,1)} async-done(((bf16[512,768]{1,0:T(8,128)(2,1)}), bf16[128,768]{1,0:T(8,128)(2,1)}) %reduce-scatter.19.cloned.1.call-update) | async-done | bytes 196624 | tf_op jit(solution)/shard_map/reduce_scatter | solution.py:85
  353.9 1.2 multiply_reduce_fusion
  355.1 1.9 fusion.43
  357.0 8.2 all_gather.37
  366.1 2.0 broadcast_in_dim.122
  368.1 2.0 broadcast_in_dim.122.clone
  370.2 58.8 %while.18 = (s32[]{:T(128)}, f32[512,3,64]{0,2,1:T(8,128)S(1)}, f32[4096,192]{0,1:T(8,128)}, f32[4096,192]{0,1:T(8,128)}, bf16[4096,192]{0,1:T(8,128)(2,1)S(1)},...) while((s32[]{:T(128)}, f32[512,3,64]{0,2,1:T(8,128)S(1)}, ...), condition=%wide.region_18.19_spmd.clone, body=%wide.region_17.18_spmd.clone.sunk | while | flops 2045968384 | bytes 107786520 | solution.py:282
  370.2 6.4 fusion.105
  377.4 7.4 fusion.106
  384.8 2.0 fusion.109
  387.4 6.1 fusion.108
  393.5 2.0 constant_dynamic-update-slice_fusion.3
  395.5 4.0 fusion.107
  399.7 6.4 fusion.105
  406.9 7.4 fusion.106
  414.3 2.0 fusion.109
  416.8 6.1 fusion.108
  422.9 2.0 constant_dynamic-update-slice_fusion.3
  424.9 4.0 fusion.107
  430.1 1.4 convolution_bitcast_fusion.1
  431.6 4.7 fusion.13
  436.4 68.1 %reduce-scatter.21.cloned.1.call-done = f32[512,192]{0,1:T(8,128)} async-done(((f32[4096,192]{0,1:T(8,128)}), f32[512,192]{0,1:T(8,128)}) %reduce-scatter.21.cloned.1.call-update) | async-done | bytes 393232 | tf_op jit(solution)/shard_map/reduce_scatter | solution.py:286
  505.8 77.0 %reduce-scatter.23.cloned.1.call-done = f32[512,192]{0,1:T(8,128)} async-done(((f32[4096,192]{0,1:T(8,128)}), f32[512,192]{0,1:T(8,128)}) %reduce-scatter.23.cloned.1.call-update) | async-done | bytes 393232 | tf_op jit(solution)/shard_map/reduce_scatter | solution.py:287
  584.5 1.7 bitcast_convert_fusion
  586.5 1.7 fusion.14
  588.3 1.8 copy.71
  590.2 2.3 fusion.51
  592.6 40.0 %all-reduce = (f32[768]{0:T(1024)}, f32[768]{0:T(1024)}, f32[768]{0:T(1024)}, f32[768]{0:T(1024)}) all-reduce(f32[768]{0:T(1024)S(1)} %get-tuple-element.293, f32[768]{0:T(1024)S(1)} %get-tuple-element.298, f32[768]{0:T(1024)S(1)} %copy-done.35, f32[768]{0:T(1024)S(1)} %copy-done.36), channel_id=1, replica_groups=mesh['row'=8,'col'=4] {'row','col'}, use_global_device_ids=true, to_apply=%region_27.28 | all-reduce | flops 3072 | bytes 24576 | tf_op jit(solution)/shard_map/psum | solution.py:310
  632.5 15.5 %reduce-scatter.33.cloned.1.call-done = f32[96,192]{1,0:T(8,128)} async-done(((f32[768,192]{1,0:T(8,128)}), f32[96,192]{1,0:T(8,128)}) %reduce-scatter.33.cloned.1.call-update) | async-done | bytes 73744
  648.0 1.6 copy.70
  649.6 96.5 %reduce-scatter.27.cloned.1.call-done = f32[96,2,768]{2,0,1:T(8,128)} async-done(((f32[768,2,768]{2,0,1:T(8,128)}), f32[96,2,768]{2,0,1:T(8,128)}) %reduce-scatter.27.cloned.1.call-update) | async-done | bytes 589840 | tf_op jit(solution)/shard_map/reduce_scatter | solution.py:307
  746.1 2.3 copy.61
  748.4 23.1 %reduce-scatter.25.cloned.1.call-done = bf16[128,768]{1,0:T(8,128)(2,1)} async-done(((bf16[512,768]{1,0:T(8,128)(2,1)}), bf16[128,768]{1,0:T(8,128)(2,1)}) %reduce-scatter.25.cloned.1.call-update) | async-done | bytes 196624 | tf_op jit(solution)/shard_map/reduce_scatter | solution.py:85
  771.5 1.7 convert_add_fusion
  773.2 68.9 %reduce-scatter.31.cloned.1.call-done = f32[96,576]{1,0:T(8,128)} async-done(((f32[768,576]{1,0:T(8,128)}), f32[96,576]{1,0:T(8,128)}) %reduce-scatter.31.cloned.1.call-update) | async-done | bytes 221200
  842.1 1.1 copy.72
  844.1 69.8 %reduce-scatter.29.cloned.1.call-done = f32[768,96]{0,1:T(8,128)} async-done(((f32[768,768]{0,1:T(8,128)}), f32[768,96]{0,1:T(8,128)}) %reduce-scatter.29.cloned.1.call-update) | async-done | bytes 294928 | tf_op jit(solution)/shard_map/reduce_scatter | solution.py:308
  (165 shorter events, 22.6 us)
Async XLA Ops:
  7.2 42.3 %copy-start.3 = (bf16[128,768]{1,0:T(8,128)(2,1)S(1)}, bf16[128,768]{1,0:T(8,128)(2,1)}, u32[]{:S(2)}) copy-start(bf16[128,768]{1,0:T(8,128)(2,1)} %param.14) | copy-start | bytes 589828
  7.2 102.1 %all-gather.6.cloned.1.call-start = ((), (), s32[]{:S(2)}) async-start(), calls=%async_computation.11 | async-start | bytes 1769472 | tf_op jit(solution)/shard_map/all_gather | solution.py:167
  49.5 11.2 %copy-start.9 = (bf16[768,3,192]{0,2,1:T(8,128)(2,1)}, bf16[768,3,192]{0,2,1:T(8,128)(2,1)S(1)}, u32[]{:S(2)}) copy-start(bf16[768,3,192]{0,2,1:T(8,128)(2,1)S(1)} %copy.55) | copy-start | bytes 2654212
  49.5 10.4 %copy-start.32 = (s32[4096]{0:T(1024)S(1)}, s32[4096]{0:T(1024)}, u32[]{:S(2)}) copy-start(s32[4096]{0:T(1024)} %param.25) | copy-start | bytes 49156
  58.3 0.9 copy-start.13
  59.2 2.7 copy-start.31
  60.6 0.6 copy-start.21
  60.6 0.6 copy-start.23
  62.8 21.9 %all-to-all-start = ((bf16[8,192,96]{2,1,0:T(8,128)(2,1)}), bf16[8,192,96]{2,1,0:T(8,128)(2,1)S(1)}, u32[]{:S(2)}, u32[]{:S(2)}) async-start(bf16[8,192,96]{2,1,0:T(8,128)(2,1)} %stack.31), calls=%async_computation | async-start | bytes 786432 | tf_op jit(solution)/shard_map/all_to_all | solution.py:17
  66.5 88.9 %all-gather.12.cloned.1.call-start = ((), (), s32[]{:S(2)}) async-start(), calls=%async_computation.22 | async-start | bytes 1769472 | tf_op jit(solution)/shard_map/all_gather | solution.py:168
  67.3 123.2 %reduce-scatter.15.cloned.1.call-start = ((), (), s32[]{:S(2)}) async-start(), calls=%async_computation.12 | async-start | bytes 983040 | tf_op jit(solution)/shard_map/reduce_scatter | solution.py:85
  155.4 13.5 %copy-start.26 = (bf16[96,2,768]{2,1,0:T(2,128)(2,1)S(1)}, bf16[96,2,768]{2,1,0:T(2,128)(2,1)}, u32[]{:S(2)}) copy-start(bf16[96,2,768]{2,1,0:T(2,128)(2,1)} %param.17) | copy-start | bytes 884740
  167.5 25.1 %copy-start.30 = (f32[768]{0:T(1024)S(1)}, f32[768]{0:T(1024)}, u32[]{:S(2)}) copy-start(f32[768]{0:T(1024)} %param.19) | copy-start | bytes 9220
  167.5 25.1 %copy-start.33 = (f32[768]{0:T(1024)S(1)}, f32[768]{0:T(1024)}, u32[]{:S(2)}) copy-start(f32[768]{0:T(1024)} %param.20) | copy-start | bytes 9220
  168.9 76.4 %all-gather.8.cloned.1.call-start = ((), (), s32[]{:S(2)}) async-start(), calls=%async_computation.13 | async-start | bytes 2654208 | tf_op jit(solution)/shard_map/all_gather | solution.py:144
  169.7 117.5 %all-gather.10.cloned.1.call-start = ((), (), s32[]{:S(2)}) async-start(), calls=%async_computation.14 | async-start | bytes 1327104 | tf_op jit(solution)/shard_map/all_gather | solution.py:145
  170.3 142.1 %reduce-scatter.17.cloned.1.call-start = ((), (), s32[]{:S(2)}) async-start(), calls=%async_computation.15 | async-start | bytes 983040 | tf_op jit(solution)/shard_map/reduce_scatter | solution.py:85
  202.1 43.2 %copy-start.18 = (bf16[512,768]{1,0:T(8,128)(2,1)}, bf16[512,768]{1,0:T(8,128)(2,1)S(1)}, u32[]{:S(2)}) copy-start(bf16[512,768]{1,0:T(8,128)(2,1)S(1)} %all_gather.33) | copy-start | bytes 2359300
  248.4 1.6 copy-start.11
  250.5 64.2 %copy-start.7 = (bf16[512,768]{1,0:T(8,128)(2,1)}, bf16[512,768]{1,0:T(8,128)(2,1)S(1)}, u32[]{:S(2)}) copy-start(bf16[512,768]{1,0:T(8,128)(2,1)S(1)} %multiply_convert_fusion.2) | copy-start | bytes 2359300
  250.5 61.9 %copy-start.6 = (bf16[128,768]{1,0:T(8,128)(2,1)S(1)}, bf16[128,768]{1,0:T(8,128)(2,1)}, u32[]{:S(2)}) copy-start(bf16[128,768]{1,0:T(8,128)(2,1)} %reduce-scatter.15.cloned.1.call-done) | copy-start | bytes 589828
  250.5 63.4 %copy-start.20 = (bf16[128,768]{1,0:T(8,128)(2,1)S(1)}, bf16[128,768]{1,0:T(8,128)(2,1)}, u32[]{:S(2)}) copy-start(bf16[128,768]{1,0:T(8,128)(2,1)} %param.23) | copy-start | bytes 589828
  250.5 63.4 %copy-start.34 = (f32[768]{0:T(1024)S(1)}, f32[768]{0:T(1024)}, u32[]{:S(2)}) copy-start(f32[768]{0:T(1024)} %param.21) | copy-start | bytes 9220
  250.5 64.2 %copy-start.37 = (f32[768]{0:T(1024)S(1)}, f32[768]{0:T(1024)}, u32[]{:S(2)}) copy-start(f32[768]{0:T(1024)} %param.22) | copy-start | bytes 9220
  290.2 63.7 %reduce-scatter.19.cloned.1.call-start = ((), (), s32[]{:S(2)}) async-start(), calls=%async_computation.16 | async-start | bytes 983040 | tf_op jit(solution)/shard_map/reduce_scatter | solution.py:85
  312.4 11.4 %copy-start.12 = (f32[512,2,768]{2,0,1:T(8,128)S(1)}, f32[512,2,768]{2,0,1:T(8,128)}, u32[]{:S(2)}) copy-start(f32[512,2,768]{2,0,1:T(8,128)} %copy-done.11) | copy-start | bytes 9437188
  323.8 2.8 copy-start.15
  323.8 3.9 copy-start.38
  326.6 0.9 copy-start.39
  326.6 1.1 copy-start.41
  330.1 35.5 %copy-start.25 = (f32[3,512,64]{1,2,0:T(8,128)S(1)}, f32[3,512,64]{1,2,0:T(8,128)}, u32[]{:S(2)}) copy-start(f32[3,512,64]{1,2,0:T(8,128)} %get-tuple-element.359) | copy-start | bytes 1179652
  330.1 174.4 %reduce-scatter.21.cloned.1.call-start = ((), (), s32[]{:S(2)}) async-start(), calls=%async_computation.17 | async-start | bytes 3538944 | tf_op jit(solution)/shard_map/reduce_scatter | solution.py:286
  365.2 0.9 copy-start.4
  366.1 4.0 copy-start.1
  370.2 7.1 copy-start.2
  384.8 2.6 copy-start
  399.7 7.1 copy-start.2
  414.2 2.6 copy-start
  429.0 1.1 copy-start.5
  429.0 2.6 copy-start.19
  429.0 2.6 copy-start.40
  429.0 153.7 %reduce-scatter.23.cloned.1.call-start = ((), (), s32[]{:S(2)}) async-start(), calls=%async_computation.18 | async-start | bytes 3538944 | tf_op jit(solution)/shard_map/reduce_scatter | solution.py:287
  429.8 218.2 %reduce-scatter.33.cloned.1.call-start = ((), (), s32[]{:S(2)}) async-start(), calls=%async_computation.24 | async-start | bytes 884736
  431.6 314.5 %reduce-scatter.27.cloned.1.call-start = ((), (), s32[]{:S(2)}) async-start(), calls=%async_computation.20 | async-start | bytes 5308416 | tf_op jit(solution)/shard_map/reduce_scatter | solution.py:307
  436.3 69.2 %copy-start.22 = (f32[512,32]{0,1:T(8,128)S(1)}, f32[512,32]{0,1:T(8,128)}, u32[]{:S(2)}) copy-start(f32[512,32]{0,1:T(8,128)} %copy-done.21) | copy-start | bytes 196612
  436.3 69.2 %copy-start.24 = (f32[512,32]{0,1:T(8,128)S(1)}, f32[512,32]{0,1:T(8,128)}, u32[]{:S(2)}) copy-start(f32[512,32]{0,1:T(8,128)} %copy-done.23) | copy-start | bytes 196612
  436.3 148.1 %copy-start.10 = (bf16[768,3,192]{0,2,1:T(8,128)(2,1)S(1)}, bf16[768,3,192]{0,2,1:T(8,128)(2,1)}, u32[]{:S(2)}) copy-start(bf16[768,3,192]{0,2,1:T(8,128)(2,1)} %copy-done.9) | copy-start | bytes 2654212
  436.3 335.2 %reduce-scatter.25.cloned.1.call-start = ((), (), s32[]{:S(2)}) async-start(), calls=%async_computation.19 | async-start | bytes 983040 | tf_op jit(solution)/shard_map/reduce_scatter | solution.py:85
  505.7 80.5 %copy-start.27 = (bf16[512,3,64]{0,2,1:T(8,128)(2,1)}, bf16[512,3,64]{0,2,1:T(8,128)(2,1)S(1)}, u32[]{:S(2)}) copy-start(bf16[512,3,64]{0,2,1:T(8,128)(2,1)S(1)} %pad_maximum_fusion.8) | copy-start | bytes 589828
  505.7 80.8 %copy-start.14 = (bf16[512,768]{1,0:T(8,128)(2,1)S(1)}, bf16[512,768]{1,0:T(8,128)(2,1)}, u32[]{:S(2)}) copy-start(bf16[512,768]{1,0:T(8,128)(2,1)} %copy-done.13) | copy-start | bytes 2359300
  505.7 80.5 %copy-start.28 = (bf16[512,3,64]{0,2,1:T(8,128)(2,1)}, bf16[512,3,64]{0,2,1:T(8,128)(2,1)S(1)}, u32[]{:S(2)}) copy-start(bf16[512,3,64]{0,2,1:T(8,128)(2,1)S(1)} %pad_maximum_fusion.9) | copy-start | bytes 589828
  583.8 0.7 copy-start.29
  586.2 255.9 %reduce-scatter.31.cloned.1.call-start = ((), (), s32[]{:S(2)}) async-start(), calls=%async_computation.23 | async-start | bytes 2211840
  588.3 2.0 copy-start.8
  588.3 2.0 copy-start.16
  590.1 2.4 copy-start.35
  590.2 2.4 copy-start.36
  590.2 323.8 %reduce-scatter.29.cloned.1.call-start = ((), (), s32[]{:S(2)}) async-start(), calls=%async_computation.21 | async-start | bytes 2654208 | tf_op jit(solution)/shard_map/reduce_scatter | solution.py:308
  592.5 179.0 %copy-start.17 = (f32[128,768]{1,0:T(8,128)S(1)}, f32[128,768]{1,0:T(8,128)}, u32[]{:S(2)}) copy-start(f32[128,768]{1,0:T(8,128)} %get-tuple-element.330) | copy-start | bytes 1179652
Sparse Core Ops, SparseCore 0:
  62.1 47.1 all-gather.5
  111.9 43.5 all-gather.11
  169.0 21.4 reduce-scatter.14
  193.3 51.9 all-gather.7
  247.6 39.5 all-gather.9
  290.3 22.0 reduce-scatter.16
  330.2 23.6 reduce-scatter.18
  429.1 75.3 reduce-scatter.20
  508.5 74.1 reduce-scatter.22
  586.3 61.6 reduce-scatter.32
  651.6 94.4 reduce-scatter.26
  748.5 23.0 reduce-scatter.24
  775.4 66.6 reduce-scatter.30
  846.1 67.8 reduce-scatter.28
